TPU v7x, 256 devices: a whole 4x4x8 slice. The times are simulated.
256 devices in a mesh: rows: 16 (over x, y_lo, core), cols: 16 (over z, y_hi).
Axes of the slice: x: 4, y: 4 (y_hi: 2, y_lo: 2; y = y_hi * 2 + y_lo), z: 8, core: 2. Of those that a mesh axis runs over, the one named last changes fastest.
Arguments:
- unary: float32 [21, 256, 2048], P(None, 'rows', 'cols'), may hold values from -8 to 300
- features: bfloat16 [64, 256, 2048], P(None, 'rows', 'cols'), may hold values from -9 to 9
- compat: float32 [21, 21], replicated, may hold values from -6 to 6
- grad_output: float32 [21, 256, 2048], P(None, 'rows', 'cols'), may hold values from -6 to 6
Outputs:
- unary_grad: float32 [21, 256, 2048], P(None, 'rows', 'cols')
- feature_grad: float32 [64, 256, 2048], P(None, 'rows', 'cols')
- compat_grad: float32 [21, 21], replicated
All inputs are finite; a program needn't handle non-finite values.
Results may differ from a plain program's by a relative error of at most 0.0003.
Values may be sent and summed in bfloat16 or wider, within the bound.
A program may use at most 128 MiB of HBM per device.

v0:
```python
import math
import jax
import jax.numpy as jnp
from jax import lax
from jax.sharding import PartitionSpec as P

ITERS = 2
THETA_PIXELS = 3.0
WINDOW_OFFSETS = [
    (row_step, col_step)
    for row_step in range(-3, 4)
    for col_step in range(-3, 4)
    if row_step != 0 or col_step != 0
]


def with_halo(block, sides, width):
    for axis, dim in sides:
        count = lax.axis_size(axis)
        forward = [(i, i + 1) for i in range(count - 1)]
        backward = [(target, source) for source, target in forward]
        low = lax.ppermute(
            lax.slice_in_dim(block, block.shape[dim] - width, None, axis=dim), axis, forward
        )
        high = lax.ppermute(lax.slice_in_dim(block, 0, width, axis=dim), axis, backward)
        block = jnp.concatenate([low, block, high], axis=dim)
    return block


def spatial_weight(row_step, col_step):
    return math.exp(
        -(row_step * row_step + col_step * col_step) / (2.0 * THETA_PIXELS * THETA_PIXELS)
    )


def shifted_view(padded, row_step, col_step, height, width_cells):
    return padded[
        :, 3 + row_step : 3 + row_step + height, 3 + col_step : 3 + col_step + width_cells
    ]


def affinity(padded_features):
    height = padded_features.shape[1] - 6
    width_cells = padded_features.shape[2] - 6
    center = shifted_view(padded_features, 0, 0, height, width_cells).astype(jnp.float32)
    factor = 1.0 / (2.0 * padded_features.shape[0])
    layers = []
    for row_step, col_step in WINDOW_OFFSETS:
        shifted = shifted_view(padded_features, row_step, col_step, height, width_cells).astype(
            jnp.float32
        )
        distance = jnp.sum((shifted - center) * (shifted - center), axis=0)
        layers.append(spatial_weight(row_step, col_step) * jnp.exp(-distance * factor))
    return jnp.stack(layers)


def message(kernel, padded):
    height = kernel.shape[1]
    width_cells = kernel.shape[2]
    total = jnp.zeros((padded.shape[0], height, width_cells), jnp.float32)
    for number, (row_step, col_step) in enumerate(WINDOW_OFFSETS):
        total = total + kernel[number][None] * shifted_view(
            padded, row_step, col_step, height, width_cells
        )
    return total


def pair_terms(grad_padded, prob_padded):
    height = grad_padded.shape[1] - 6
    width_cells = grad_padded.shape[2] - 6
    grad_center = shifted_view(grad_padded, 0, 0, height, width_cells)
    prob_center = shifted_view(prob_padded, 0, 0, height, width_cells)
    layers = []
    for row_step, col_step in WINDOW_OFFSETS:
        prob_shift = shifted_view(prob_padded, row_step, col_step, height, width_cells)
        grad_shift = shifted_view(grad_padded, row_step, col_step, height, width_cells)
        layers.append(jnp.sum(grad_center * prob_shift + grad_shift * prob_center, axis=0))
    return jnp.stack(layers)


def feature_term(coefs, kernel, padded_features):
    height = kernel.shape[1]
    width_cells = kernel.shape[2]
    center = shifted_view(padded_features, 0, 0, height, width_cells).astype(jnp.float32)
    factor = 1.0 / padded_features.shape[0]
    total = jnp.zeros(center.shape, jnp.float32)
    for number, (row_step, col_step) in enumerate(WINDOW_OFFSETS):
        shifted = shifted_view(padded_features, row_step, col_step, height, width_cells).astype(
            jnp.float32
        )
        weight_map = coefs[number] * kernel[number] * factor
        total = total + weight_map[None] * (shifted - center)
    return total


def mix(compat, values):
    return jnp.einsum("cd,dhw->chw", compat, values, precision=lax.Precision.HIGHEST)


def mix_back(compat, values):
    return jnp.einsum("cd,chw->dhw", compat, values, precision=lax.Precision.HIGHEST)


def outer_sum(left, right):
    return jnp.einsum("chw,dhw->cd", left, right, precision=lax.Precision.HIGHEST)


def softmax_grad(prob, cotangent):
    return prob * (cotangent - jnp.sum(cotangent * prob, axis=0, keepdims=True))


def on_device(unary, features, compat, grad_output):
    height = unary.shape[1]
    width_cells = unary.shape[2]
    total_pixels = height * lax.axis_size("rows") * width_cells * lax.axis_size("cols")
    reach = 0
    feat_wide = with_halo(features, (("rows", 1), ("cols", 2)), 3)
    cotangent = grad_output
    start_prob = jax.nn.softmax(unary, axis=0)
    kern_store = affinity(feat_wide)

    def kernel_at():
        return kern_store

    prob_list = [start_prob]
    pad_list = [reach]
    wide_list = []
    message_list = []
    for step in range(ITERS):
        current = prob_list[-1]
        prob_wide = with_halo(current, (("rows", 1), ("cols", 2)), 3)
        wide_pad = 3
        wide_list.append((prob_wide, wide_pad))
        out_pad = wide_pad - 3
        message_out = message(kernel_at(), prob_wide)
        message_list.append(message_out)
        logits = unary - mix(compat, message_out)
        next_prob = jax.nn.softmax(logits, axis=0)
        prob_list.append(next_prob)
        pad_list.append(out_pad)
    unary_sum = jnp.zeros(unary.shape, jnp.float32)
    compat_sum = jnp.zeros(compat.shape, jnp.float32)
    coefs = jnp.zeros((len(WINDOW_OFFSETS), height, width_cells), jnp.float32)
    for step in reversed(range(ITERS)):
        later_prob = prob_list[step + 1]
        logit_grad = softmax_grad(later_prob, cotangent)
        unary_sum = unary_sum + logit_grad
        compat_sum = compat_sum - outer_sum(logit_grad, message_list[step])
        msg_grad = -mix_back(compat, logit_grad)
        grad_wide = with_halo(msg_grad, (("rows", 1), ("cols", 2)), 3)
        cotangent = message(kernel_at(), grad_wide)
        prob_wide, wide_pad = wide_list[step]
        coefs = coefs + pair_terms(grad_wide, prob_wide)
    unary_grad = unary_sum + softmax_grad(prob_list[0], cotangent)
    feature_grad = feature_term(coefs, kernel_at(), feat_wide)
    compat_grad = lax.psum(compat_sum, ("rows", "cols")) / math.sqrt(total_pixels)
    return (unary_grad, feature_grad, compat_grad)


def solution(mesh):
    placed = (P(None, "rows", "cols"), P(None, "rows", "cols"), P(), P(None, "rows", "cols"))
    return jax.shard_map(
        on_device,
        mesh=mesh,
        in_specs=placed,
        out_specs=(P(None, "rows", "cols"), P(None, "rows", "cols"), P()),
        check_vma=False,
    )
```

profile of v0, /device:TPU:33, one launch (start us, length us, event | category | flops | bytes accessed | tf_op | source)
XLA Modules:
  0.0 314.2 jit_solution(16345287022579159694)
XLA Ops:
  3.7 3.8 %collective-permute-start.3 = (f32[21,3,128]{2,0,1:T(8,128)S(1)}, f32[21,3,128]{2,0,1:T(8,128)S(1)}, u32[]{:S(2)}, u32[]{:S(2)}) collective-permute-start(f32[21,3,128]{2,0,1:T(8,128)S(1)} %get-tuple-element.238), channel_id=1, source_target_pairs={{0,16},{16,32},{32,48},{48,64},{64,80},{80,96},{96,112},{112,128},... | collective-permute-start | bytes 96776 | tf_op jit(solution)/shard_map/ppermute | solution.py:22
  7.5 1.9 collective-permute-start.4
  9.5 3.6 %collective-permute-start = (bf16[64,3,128]{2,1,0:T(4,128)(2,1)S(1)}, bf16[64,3,128]{2,1,0:T(4,128)(2,1)S(1)}, u32[]{:S(2)}, u32[]{:S(2)}) collective-permute-start(bf16[64,3,128]{2,1,0:T(4,128)(2,1)S(1)} %get-tuple-element.229), channel_id=1, source_target_pairs={{0,16},{16,32},{32,48},{48,64},{64,80},{80,96},{96,112},{112,128},... | collective-permute-start | bytes 147464 | tf_op jit(solution)/shard_map/ppermute | solution.py:22
  13.1 1.9 collective-permute-start.1
  15.2 4.5 %collective-permute-start.5 = (f32[21,22,3]{2,0,1:T(8,128)S(1)}, f32[21,22,3]{2,0,1:T(8,128)S(1)}, u32[]{:S(2)}, u32[]{:S(2)}) collective-permute-start(f32[21,22,3]{2,0,1:T(8,128)S(1)} %get-tuple-element.227), channel_id=1, source_target_pairs={{0,1},{1,2},{2,3},{3,4},{4,5},{5,6},{6,7},{7,8},{8,9},{9,10},{10,1... | collective-permute-start | bytes 16640 | tf_op jit(solution)/shard_map/ppermute | solution.py:22
  19.8 3.2 %collective-permute-start.7 = (f32[21,22,3]{2,0,1:T(8,128)S(1)}, f32[21,22,3]{2,0,1:T(8,128)S(1)}, u32[]{:S(2)}, u32[]{:S(2)}) collective-permute-start(f32[21,22,3]{2,0,1:T(8,128)S(1)} %get-tuple-element.228), channel_id=1, source_target_pairs={{1,0},{2,1},{3,2},{4,3},{5,4},{6,5},{7,6},{8,7},{9,8},{10,9},{11,1... | collective-permute-start | bytes 16640 | tf_op jit(solution)/shard_map/ppermute | solution.py:25
  23.0 8.2 %collective-permute-done.5 = f32[21,22,3]{2,0,1:T(8,128)S(1)} collective-permute-done((f32[21,22,3]{2,0,1:T(8,128)S(1)}, f32[21,22,3]{2,0,1:T(8,128)S(1)}, u32[]{:S(2)}, u32[]{:S(2)}) %collective-permute-start.5) | collective-permute-done | bytes 5576 | tf_op jit(solution)/shard_map/ppermute | solution.py:22
  31.1 1.9 collective-permute-done.7
  33.7 3.0 collective-permute-start.6
  36.7 3.8 %collective-permute-start.2 = (bf16[64,22,3]{2,1,0:T(8,128)(2,1)S(1)}, bf16[64,22,3]{2,1,0:T(8,128)(2,1)S(1)}, u32[]{:S(2)}, u32[]{:S(2)}) collective-permute-start(bf16[64,22,3]{2,1,0:T(8,128)(2,1)S(1)} %get-tuple-element.212), channel_id=1, source_target_pairs={{0,1},{1,2},{2,3},{3,4},{4,5},{5,6},{6,7},{7,8},{8,9},{9,10},{10,1... | collective-permute-start | bytes 25352 | tf_op jit(solution)/shard_map/ppermute | solution.py:22
  40.5 15.3 %collective-permute-done.6 = bf16[64,22,3]{2,1,0:T(8,128)(2,1)S(1)} collective-permute-done((bf16[64,22,3]{2,1,0:T(8,128)(2,1)S(1)}, bf16[64,22,3]{2,1,0:T(8,128)(2,1)S(1)}, u32[]{:S(2)}, u32[]{:S(2)}) %collective-permute-start.6) | collective-permute-done | bytes 8480 | tf_op jit(solution)/shard_map/ppermute | solution.py:25
  56.9 2.4 multiply_reduce_fusion.43
  59.5 2.9 multiply_reduce_fusion.47
  62.4 2.6 multiply_reduce_fusion.46
  79.6 2.7 multiply_add_fusion.4
  83.4 5.8 %collective-permute-start.8 = (f32[21,3,128]{2,0,1:T(8,128)S(1)}, f32[21,3,128]{2,0,1:T(8,128)S(1)}, u32[]{:S(2)}, u32[]{:S(2)}) collective-permute-start(f32[21,3,128]{2,0,1:T(8,128)S(1)} %get-tuple-element.236), channel_id=1, source_target_pairs={{0,16},{16,32},{32,48},{48,64},{64,80},{80,96},{96,112},{112,128},... | collective-permute-start | bytes 96776 | tf_op jit(solution)/shard_map/ppermute | solution.py:22
  89.2 1.9 collective-permute-start.9
  91.1 3.3 %collective-permute-done.9 = f32[21,3,128]{2,0,1:T(8,128)S(1)} collective-permute-done((f32[21,3,128]{2,0,1:T(8,128)S(1)}, f32[21,3,128]{2,0,1:T(8,128)S(1)}, u32[]{:S(2)}, u32[]{:S(2)}) %collective-permute-start.9) | collective-permute-done | bytes 32288 | tf_op jit(solution)/shard_map/ppermute | solution.py:25
  94.6 4.8 %collective-permute-start.10 = (f32[21,22,3]{2,0,1:T(8,128)S(1)}, f32[21,22,3]{2,0,1:T(8,128)S(1)}, u32[]{:S(2)}, u32[]{:S(2)}) collective-permute-start(f32[21,22,3]{2,0,1:T(8,128)S(1)} %get-tuple-element.223), channel_id=1, source_target_pairs={{0,1},{1,2},{2,3},{3,4},{4,5},{5,6},{6,7},{7,8},{8,9},{9,10},{10,1... | collective-permute-start | bytes 16640 | tf_op jit(solution)/shard_map/ppermute | solution.py:22
  99.4 3.0 collective-permute-start.11
  102.5 7.3 %collective-permute-done.10 = f32[21,22,3]{2,0,1:T(8,128)S(1)} collective-permute-done((f32[21,22,3]{2,0,1:T(8,128)S(1)}, f32[21,22,3]{2,0,1:T(8,128)S(1)}, u32[]{:S(2)}, u32[]{:S(2)}) %collective-permute-start.10) | collective-permute-done | bytes 5576 | tf_op jit(solution)/shard_map/ppermute | solution.py:22
  109.8 1.6 collective-permute-done.11
  111.6 2.8 multiply_add_fusion.3
  116.0 1.4 fusion.19
  118.5 4.6 %collective-permute-start.12 = (f32[21,3,128]{2,0,1:T(8,128)S(1)}, f32[21,3,128]{2,0,1:T(8,128)S(1)}, u32[]{:S(2)}, u32[]{:S(2)}) collective-permute-start(f32[21,3,128]{2,0,1:T(8,128)S(1)} %get-tuple-element.234), channel_id=1, source_target_pairs={{0,16},{16,32},{32,48},{48,64},{64,80},{80,96},{96,112},{112,128},... | collective-permute-start | bytes 96776 | tf_op jit(solution)/shard_map/ppermute | solution.py:22
  123.0 1.9 collective-permute-start.13
  125.0 3.3 %collective-permute-done.13 = f32[21,3,128]{2,0,1:T(8,128)S(1)} collective-permute-done((f32[21,3,128]{2,0,1:T(8,128)S(1)}, f32[21,3,128]{2,0,1:T(8,128)S(1)}, u32[]{:S(2)}, u32[]{:S(2)}) %collective-permute-start.13) | collective-permute-done | bytes 32288 | tf_op jit(solution)/shard_map/ppermute | solution.py:25
  128.5 3.9 %collective-permute-start.14 = (f32[21,22,3]{2,0,1:T(8,128)S(1)}, f32[21,22,3]{2,0,1:T(8,128)S(1)}, u32[]{:S(2)}, u32[]{:S(2)}) collective-permute-start(f32[21,22,3]{2,0,1:T(8,128)S(1)} %get-tuple-element.219), channel_id=1, source_target_pairs={{0,1},{1,2},{2,3},{3,4},{4,5},{5,6},{6,7},{7,8},{8,9},{9,10},{10,1... | collective-permute-start | bytes 16640 | tf_op jit(solution)/shard_map/ppermute | solution.py:22
  132.4 3.8 %collective-permute-start.15 = (f32[21,22,3]{2,0,1:T(8,128)S(1)}, f32[21,22,3]{2,0,1:T(8,128)S(1)}, u32[]{:S(2)}, u32[]{:S(2)}) collective-permute-start(f32[21,22,3]{2,0,1:T(8,128)S(1)} %get-tuple-element.220), channel_id=1, source_target_pairs={{1,0},{2,1},{3,2},{4,3},{5,4},{6,5},{7,6},{8,7},{9,8},{10,9},{11,1... | collective-permute-start | bytes 16640 | tf_op jit(solution)/shard_map/ppermute | solution.py:25
  136.9 5.8 %collective-permute-done.14 = f32[21,22,3]{2,0,1:T(8,128)S(1)} collective-permute-done((f32[21,22,3]{2,0,1:T(8,128)S(1)}, f32[21,22,3]{2,0,1:T(8,128)S(1)}, u32[]{:S(2)}, u32[]{:S(2)}) %collective-permute-start.14) | collective-permute-done | bytes 5576 | tf_op jit(solution)/shard_map/ppermute | solution.py:22
  142.7 2.5 collective-permute-done.15
  146.7 1.5 add_reduce_fusion.64
  152.1 4.4 %add_reduce_fusion.48 = (f32[16,128]{1,0:T(8,128)}, f32[16,128]{1,0:T(8,128)}, f32[16,128]{1,0:T(8,128)}, f32[16,128]{1,0:T(8,128)}, f32[16,128]{1,0:T(8,128)}, ...) fusion(f32[21,16,128]{2,0,1:T(8,128)S(1)} %fusion.11, ...), kind=kLoop, calls=%fused_computation.349 | loop fusion | flops 5830656 | bytes 9657344 | tf_op jit(solution)/shard_map/reduce_sum | solution.py:77
  159.8 81.1 %psum.7 = f32[21,21]{1,0:T(8,128)S(1)} all-reduce(f32[21,21]{1,0:T(8,128)S(1)} %fusion.15), channel_id=1, replica_groups=mesh['rows'=16,'cols'=16] {'rows','cols'}, use_global_device_ids=true, to_apply=%region_153.0 | all-reduce | flops 441 | bytes 3528 | tf_op jit(solution)/shard_map/psum | solution.py:156
  241.5 1.9 collective-permute-start.16
  243.5 2.4 collective-permute-start.17
  257.8 3.8 %collective-permute-start.18 = (f32[21,22,3]{2,0,1:T(8,128)S(1)}, f32[21,22,3]{2,0,1:T(8,128)S(1)}, u32[]{:S(2)}, u32[]{:S(2)}) collective-permute-start(f32[21,22,3]{2,0,1:T(8,128)S(1)} %get-tuple-element.215), channel_id=1, source_target_pairs={{0,1},{1,2},{2,3},{3,4},{4,5},{5,6},{6,7},{7,8},{8,9},{9,10},{10,1... | collective-permute-start | bytes 16640 | tf_op jit(solution)/shard_map/ppermute | solution.py:22
  261.6 4.1 %collective-permute-start.19 = (f32[21,22,3]{2,0,1:T(8,128)S(1)}, f32[21,22,3]{2,0,1:T(8,128)S(1)}, u32[]{:S(2)}, u32[]{:S(2)}) collective-permute-start(f32[21,22,3]{2,0,1:T(8,128)S(1)} %get-tuple-element.216), channel_id=1, source_target_pairs={{1,0},{2,1},{3,2},{4,3},{5,4},{6,5},{7,6},{8,7},{9,8},{10,9},{11,1... | collective-permute-start | bytes 16640 | tf_op jit(solution)/shard_map/ppermute | solution.py:25
  266.0 6.7 %collective-permute-done.18 = f32[21,22,3]{2,0,1:T(8,128)S(1)} collective-permute-done((f32[21,22,3]{2,0,1:T(8,128)S(1)}, f32[21,22,3]{2,0,1:T(8,128)S(1)}, u32[]{:S(2)}, u32[]{:S(2)}) %collective-permute-start.18) | collective-permute-done | bytes 5576 | tf_op jit(solution)/shard_map/ppermute | solution.py:22
  272.7 3.5 %collective-permute-done.19 = f32[21,22,3]{2,0,1:T(8,128)S(1)} collective-permute-done((f32[21,22,3]{2,0,1:T(8,128)S(1)}, f32[21,22,3]{2,0,1:T(8,128)S(1)}, u32[]{:S(2)}, u32[]{:S(2)}) %collective-permute-start.19) | collective-permute-done | bytes 5576 | tf_op jit(solution)/shard_map/ppermute | solution.py:25
  281.8 1.4 fusion.129
  283.2 1.4 fusion.131
  284.7 1.4 fusion.133
  286.2 1.4 fusion.135
  287.6 1.4 fusion.137
  289.1 1.5 fusion.139
  290.9 13.9 %fusion.7 = f32[21,16,128]{2,0,1:T(8,128)S(1)} fusion(f32[21,16,128]{2,0,1:T(8,128)S(1)} %copy-done.10, f32[16,128]{1,0:T(8,128)} %fusion.19, f32[21,16,128]{2,1,0:T(8,128)} %param.7, f32[21,16,128]{2,0,1:T(8,128)} %copy-done.11, f32[16,128]{1,0:T(8,128)} %get-tuple-element.242, f32[16,128]{1,0:T(8,128)S(1)} %copy-done.13, f32[16,128]{1,0:T(8,128)S(1)} %reduce_max.27, ...), kind=kOutput, calls=%fused_computation.55 | output fusion | flops 9205780 | bytes 18972672 | tf_op jit(solution)/shard_map/sub | solution.py:109
  305.9 8.3 %multiply_add_fusion = f32[64,16,128]{2,1,0:T(8,128)} fusion(bf16[64,16,128]{2,1,0:T(8,128)(2,1)S(1)} %copy-done.6, bf16[64,3,128]{2,1,0:T(4,128)(2,1)S(1)} %collective-permute-done, f32[16,128]{1,0:T(8,128)} %get-tuple-element.162, f32[16,128]{1,0:T(8,128)} %get-tuple-element.163, f32[16,128]{1,0:T(8,128)} %get-tuple-element.164, ...), kind=kLoop, calls=%fused_computation.80 | loop fusion | flops 26345472 | bytes 13025280 | tf_op jit(solution)/shard_map/add | solution.py:92
  (492 shorter events, 50.4 us)
Async XLA Ops:
  3.7 11.4 %collective-permute-start.3 = (f32[21,3,128]{2,0,1:T(8,128)S(1)}, f32[21,3,128]{2,0,1:T(8,128)S(1)}, u32[]{:S(2)}, u32[]{:S(2)}) collective-permute-start(f32[21,3,128]{2,0,1:T(8,128)S(1)} %get-tuple-element.238), channel_id=1, source_target_pairs={{0,16},{16,32},{32,48},{48,64},{64,80},{80,96},{96,112},{112,128},... | collective-permute-start | bytes 96776 | tf_op jit(solution)/shard_map/ppermute | solution.py:22
  7.5 7.6 %collective-permute-start.4 = (f32[21,3,128]{2,0,1:T(8,128)S(1)}, f32[21,3,128]{2,0,1:T(8,128)S(1)}, u32[]{:S(2)}, u32[]{:S(2)}) collective-permute-start(f32[21,3,128]{2,0,1:T(8,128)S(1)} %get-tuple-element.239), channel_id=1, source_target_pairs={{16,0},{32,16},{48,32},{64,48},{80,64},{96,80},{112,96},{128,112},... | collective-permute-start | bytes 96776 | tf_op jit(solution)/shard_map/ppermute | solution.py:25
  9.5 23.8 %collective-permute-start = (bf16[64,3,128]{2,1,0:T(4,128)(2,1)S(1)}, bf16[64,3,128]{2,1,0:T(4,128)(2,1)S(1)}, u32[]{:S(2)}, u32[]{:S(2)}) collective-permute-start(bf16[64,3,128]{2,1,0:T(4,128)(2,1)S(1)} %get-tuple-element.229), channel_id=1, source_target_pairs={{0,16},{16,32},{32,48},{48,64},{64,80},{80,96},{96,112},{112,128},... | collective-permute-start | bytes 147464 | tf_op jit(solution)/shard_map/ppermute | solution.py:22
  13.1 20.1 %collective-permute-start.1 = (bf16[64,3,128]{2,1,0:T(4,128)(2,1)S(1)}, bf16[64,3,128]{2,1,0:T(4,128)(2,1)S(1)}, u32[]{:S(2)}, u32[]{:S(2)}) collective-permute-start(bf16[64,3,128]{2,1,0:T(4,128)(2,1)S(1)} %get-tuple-element.230), channel_id=1, source_target_pairs={{16,0},{32,16},{48,32},{64,48},{80,64},{96,80},{112,96},{128,112},... | collective-permute-start | bytes 147464 | tf_op jit(solution)/shard_map/ppermute | solution.py:25
  15.2 15.9 %collective-permute-start.5 = (f32[21,22,3]{2,0,1:T(8,128)S(1)}, f32[21,22,3]{2,0,1:T(8,128)S(1)}, u32[]{:S(2)}, u32[]{:S(2)}) collective-permute-start(f32[21,22,3]{2,0,1:T(8,128)S(1)} %get-tuple-element.227), channel_id=1, source_target_pairs={{0,1},{1,2},{2,3},{3,4},{4,5},{5,6},{6,7},{7,8},{8,9},{9,10},{10,1... | collective-permute-start | bytes 16640 | tf_op jit(solution)/shard_map/ppermute | solution.py:22
  19.8 13.3 %collective-permute-start.7 = (f32[21,22,3]{2,0,1:T(8,128)S(1)}, f32[21,22,3]{2,0,1:T(8,128)S(1)}, u32[]{:S(2)}, u32[]{:S(2)}) collective-permute-start(f32[21,22,3]{2,0,1:T(8,128)S(1)} %get-tuple-element.228), channel_id=1, source_target_pairs={{1,0},{2,1},{3,2},{4,3},{5,4},{6,5},{7,6},{8,7},{9,8},{10,9},{11,1... | collective-permute-start | bytes 16640 | tf_op jit(solution)/shard_map/ppermute | solution.py:25
  33.7 22.1 %collective-permute-start.6 = (bf16[64,22,3]{2,1,0:T(8,128)(2,1)S(1)}, bf16[64,22,3]{2,1,0:T(8,128)(2,1)S(1)}, u32[]{:S(2)}, u32[]{:S(2)}) collective-permute-start(bf16[64,22,3]{2,1,0:T(8,128)(2,1)S(1)} %get-tuple-element.211), channel_id=1, source_target_pairs={{1,0},{2,1},{3,2},{4,3},{5,4},{6,5},{7,6},{8,7},{9,8},{10,9},{11,1... | collective-permute-start | bytes 25352 | tf_op jit(solution)/shard_map/ppermute | solution.py:25
  36.7 19.1 %collective-permute-start.2 = (bf16[64,22,3]{2,1,0:T(8,128)(2,1)S(1)}, bf16[64,22,3]{2,1,0:T(8,128)(2,1)S(1)}, u32[]{:S(2)}, u32[]{:S(2)}) collective-permute-start(bf16[64,22,3]{2,1,0:T(8,128)(2,1)S(1)} %get-tuple-element.212), channel_id=1, source_target_pairs={{0,1},{1,2},{2,3},{3,4},{4,5},{5,6},{6,7},{7,8},{8,9},{9,10},{10,1... | collective-permute-start | bytes 25352 | tf_op jit(solution)/shard_map/ppermute | solution.py:22
  83.4 7.7 %collective-permute-start.8 = (f32[21,3,128]{2,0,1:T(8,128)S(1)}, f32[21,3,128]{2,0,1:T(8,128)S(1)}, u32[]{:S(2)}, u32[]{:S(2)}) collective-permute-start(f32[21,3,128]{2,0,1:T(8,128)S(1)} %get-tuple-element.236), channel_id=1, source_target_pairs={{0,16},{16,32},{32,48},{48,64},{64,80},{80,96},{96,112},{112,128},... | collective-permute-start | bytes 96776 | tf_op jit(solution)/shard_map/ppermute | solution.py:22
  89.2 5.3 %collective-permute-start.9 = (f32[21,3,128]{2,0,1:T(8,128)S(1)}, f32[21,3,128]{2,0,1:T(8,128)S(1)}, u32[]{:S(2)}, u32[]{:S(2)}) collective-permute-start(f32[21,3,128]{2,0,1:T(8,128)S(1)} %get-tuple-element.237), channel_id=1, source_target_pairs={{16,0},{32,16},{48,32},{64,48},{80,64},{96,80},{112,96},{128,112},... | collective-permute-start | bytes 96776 | tf_op jit(solution)/shard_map/ppermute | solution.py:25
  94.6 15.2 %collective-permute-start.10 = (f32[21,22,3]{2,0,1:T(8,128)S(1)}, f32[21,22,3]{2,0,1:T(8,128)S(1)}, u32[]{:S(2)}, u32[]{:S(2)}) collective-permute-start(f32[21,22,3]{2,0,1:T(8,128)S(1)} %get-tuple-element.223), channel_id=1, source_target_pairs={{0,1},{1,2},{2,3},{3,4},{4,5},{5,6},{6,7},{7,8},{8,9},{9,10},{10,1... | collective-permute-start | bytes 16640 | tf_op jit(solution)/shard_map/ppermute | solution.py:22
  99.4 12.0 %collective-permute-start.11 = (f32[21,22,3]{2,0,1:T(8,128)S(1)}, f32[21,22,3]{2,0,1:T(8,128)S(1)}, u32[]{:S(2)}, u32[]{:S(2)}) collective-permute-start(f32[21,22,3]{2,0,1:T(8,128)S(1)} %get-tuple-element.224), channel_id=1, source_target_pairs={{1,0},{2,1},{3,2},{4,3},{5,4},{6,5},{7,6},{8,7},{9,8},{10,9},{11,1... | collective-permute-start | bytes 16640 | tf_op jit(solution)/shard_map/ppermute | solution.py:25
  118.5 6.5 %collective-permute-start.12 = (f32[21,3,128]{2,0,1:T(8,128)S(1)}, f32[21,3,128]{2,0,1:T(8,128)S(1)}, u32[]{:S(2)}, u32[]{:S(2)}) collective-permute-start(f32[21,3,128]{2,0,1:T(8,128)S(1)} %get-tuple-element.234), channel_id=1, source_target_pairs={{0,16},{16,32},{32,48},{48,64},{64,80},{80,96},{96,112},{112,128},... | collective-permute-start | bytes 96776 | tf_op jit(solution)/shard_map/ppermute | solution.py:22
  123.0 5.3 %collective-permute-start.13 = (f32[21,3,128]{2,0,1:T(8,128)S(1)}, f32[21,3,128]{2,0,1:T(8,128)S(1)}, u32[]{:S(2)}, u32[]{:S(2)}) collective-permute-start(f32[21,3,128]{2,0,1:T(8,128)S(1)} %get-tuple-element.235), channel_id=1, source_target_pairs={{16,0},{32,16},{48,32},{64,48},{80,64},{96,80},{112,96},{128,112},... | collective-permute-start | bytes 96776 | tf_op jit(solution)/shard_map/ppermute | solution.py:25
  128.5 14.3 %collective-permute-start.14 = (f32[21,22,3]{2,0,1:T(8,128)S(1)}, f32[21,22,3]{2,0,1:T(8,128)S(1)}, u32[]{:S(2)}, u32[]{:S(2)}) collective-permute-start(f32[21,22,3]{2,0,1:T(8,128)S(1)} %get-tuple-element.219), channel_id=1, source_target_pairs={{0,1},{1,2},{2,3},{3,4},{4,5},{5,6},{6,7},{7,8},{8,9},{9,10},{10,1... | collective-permute-start | bytes 16640 | tf_op jit(solution)/shard_map/ppermute | solution.py:22
  132.4 12.9 %collective-permute-start.15 = (f32[21,22,3]{2,0,1:T(8,128)S(1)}, f32[21,22,3]{2,0,1:T(8,128)S(1)}, u32[]{:S(2)}, u32[]{:S(2)}) collective-permute-start(f32[21,22,3]{2,0,1:T(8,128)S(1)} %get-tuple-element.220), channel_id=1, source_target_pairs={{1,0},{2,1},{3,2},{4,3},{5,4},{6,5},{7,6},{8,7},{9,8},{10,9},{11,1... | collective-permute-start | bytes 16640 | tf_op jit(solution)/shard_map/ppermute | solution.py:25
  158.0 97.6 %copy-start.138 = (f32[16,128]{1,0:T(8,128)S(1)}, f32[16,128]{1,0:T(8,128)}, u32[]{:S(2)}) copy-start(f32[16,128]{1,0:T(8,128)} %get-tuple-element.144) | copy-start | bytes 24580
  158.4 97.2 %copy-start.149 = (f32[16,128]{1,0:T(8,128)S(1)}, f32[16,128]{1,0:T(8,128)}, u32[]{:S(2)}) copy-start(f32[16,128]{1,0:T(8,128)} %get-tuple-element.28) | copy-start | bytes 24580
  158.4 97.2 %copy-start.148 = (f32[16,128]{1,0:T(8,128)S(1)}, f32[16,128]{1,0:T(8,128)}, u32[]{:S(2)}) copy-start(f32[16,128]{1,0:T(8,128)} %get-tuple-element.27) | copy-start | bytes 24580
  158.4 97.3 %copy-start.147 = (f32[16,128]{1,0:T(8,128)S(1)}, f32[16,128]{1,0:T(8,128)}, u32[]{:S(2)}) copy-start(f32[16,128]{1,0:T(8,128)} %get-tuple-element.26) | copy-start | bytes 24580
  158.4 98.7 %copy-start.154 = (f32[16,128]{1,0:T(8,128)S(1)}, f32[16,128]{1,0:T(8,128)}, u32[]{:S(2)}) copy-start(f32[16,128]{1,0:T(8,128)} %get-tuple-element.31) | copy-start | bytes 24580
  158.5 98.7 %copy-start.143 = (f32[16,128]{1,0:T(8,128)S(1)}, f32[16,128]{1,0:T(8,128)}, u32[]{:S(2)}) copy-start(f32[16,128]{1,0:T(8,128)} %get-tuple-element.25) | copy-start | bytes 24580
  158.5 98.7 %copy-start.141 = (f32[16,128]{1,0:T(8,128)S(1)}, f32[16,128]{1,0:T(8,128)}, u32[]{:S(2)}) copy-start(f32[16,128]{1,0:T(8,128)} %get-tuple-element.24) | copy-start | bytes 24580
  158.5 98.7 %copy-start.139 = (f32[16,128]{1,0:T(8,128)S(1)}, f32[16,128]{1,0:T(8,128)}, u32[]{:S(2)}) copy-start(f32[16,128]{1,0:T(8,128)} %get-tuple-element.23) | copy-start | bytes 24580
  158.5 98.7 %copy-start.151 = (f32[16,128]{1,0:T(8,128)S(1)}, f32[16,128]{1,0:T(8,128)}, u32[]{:S(2)}) copy-start(f32[16,128]{1,0:T(8,128)} %get-tuple-element.30) | copy-start | bytes 24580
  158.5 98.7 %copy-start.142 = (f32[16,128]{1,0:T(8,128)S(1)}, f32[16,128]{1,0:T(8,128)}, u32[]{:S(2)}) copy-start(f32[16,128]{1,0:T(8,128)} %get-tuple-element.21) | copy-start | bytes 24580
  158.5 98.7 %copy-start.140 = (f32[16,128]{1,0:T(8,128)S(1)}, f32[16,128]{1,0:T(8,128)}, u32[]{:S(2)}) copy-start(f32[16,128]{1,0:T(8,128)} %get-tuple-element.20) | copy-start | bytes 24580
  158.5 98.7 %copy-start.152 = (f32[16,128]{1,0:T(8,128)S(1)}, f32[16,128]{1,0:T(8,128)}, u32[]{:S(2)}) copy-start(f32[16,128]{1,0:T(8,128)} %get-tuple-element.143) | copy-start | bytes 24580
  158.5 98.7 %copy-start.133 = (f32[16,128]{1,0:T(8,128)S(1)}, f32[16,128]{1,0:T(8,128)}, u32[]{:S(2)}) copy-start(f32[16,128]{1,0:T(8,128)} %get-tuple-element.22) | copy-start | bytes 24580
  158.5 98.7 %copy-start.145 = (f32[16,128]{1,0:T(8,128)S(1)}, f32[16,128]{1,0:T(8,128)}, u32[]{:S(2)}) copy-start(f32[16,128]{1,0:T(8,128)} %get-tuple-element.13) | copy-start | bytes 24580
  158.5 98.7 %copy-start.144 = (f32[16,128]{1,0:T(8,128)S(1)}, f32[16,128]{1,0:T(8,128)}, u32[]{:S(2)}) copy-start(f32[16,128]{1,0:T(8,128)} %get-tuple-element.12) | copy-start | bytes 24580
  158.6 98.8 %copy-start.134 = (f32[16,128]{1,0:T(8,128)S(1)}, f32[16,128]{1,0:T(8,128)}, u32[]{:S(2)}) copy-start(f32[16,128]{1,0:T(8,128)} %get-tuple-element.19) | copy-start | bytes 24580
  158.6 98.8 %copy-start.132 = (f32[16,128]{1,0:T(8,128)S(1)}, f32[16,128]{1,0:T(8,128)}, u32[]{:S(2)}) copy-start(f32[16,128]{1,0:T(8,128)} %get-tuple-element.18) | copy-start | bytes 24580
  158.6 98.8 %copy-start.131 = (f32[16,128]{1,0:T(8,128)S(1)}, f32[16,128]{1,0:T(8,128)}, u32[]{:S(2)}) copy-start(f32[16,128]{1,0:T(8,128)} %get-tuple-element.17) | copy-start | bytes 24580
  158.6 98.8 %copy-start.146 = (f32[16,128]{1,0:T(8,128)S(1)}, f32[16,128]{1,0:T(8,128)}, u32[]{:S(2)}) copy-start(f32[16,128]{1,0:T(8,128)} %get-tuple-element.142) | copy-start | bytes 24580
  158.6 98.8 %copy-start.137 = (f32[16,128]{1,0:T(8,128)S(1)}, f32[16,128]{1,0:T(8,128)}, u32[]{:S(2)}) copy-start(f32[16,128]{1,0:T(8,128)} %get-tuple-element.11) | copy-start | bytes 24580
  158.6 98.8 %copy-start.136 = (f32[16,128]{1,0:T(8,128)S(1)}, f32[16,128]{1,0:T(8,128)}, u32[]{:S(2)}) copy-start(f32[16,128]{1,0:T(8,128)} %get-tuple-element.10) | copy-start | bytes 24580
  158.6 98.8 %copy-start.135 = (f32[16,128]{1,0:T(8,128)S(1)}, f32[16,128]{1,0:T(8,128)}, u32[]{:S(2)}) copy-start(f32[16,128]{1,0:T(8,128)} %get-tuple-element.9) | copy-start | bytes 24580
  158.6 98.8 %copy-start.127 = (f32[16,128]{1,0:T(8,128)S(1)}, f32[16,128]{1,0:T(8,128)}, u32[]{:S(2)}) copy-start(f32[16,128]{1,0:T(8,128)} %get-tuple-element.16) | copy-start | bytes 24580
  158.6 98.8 %copy-start.126 = (f32[16,128]{1,0:T(8,128)S(1)}, f32[16,128]{1,0:T(8,128)}, u32[]{:S(2)}) copy-start(f32[16,128]{1,0:T(8,128)} %get-tuple-element.15) | copy-start | bytes 24580
  158.6 98.9 %copy-start.125 = (f32[16,128]{1,0:T(8,128)S(1)}, f32[16,128]{1,0:T(8,128)}, u32[]{:S(2)}) copy-start(f32[16,128]{1,0:T(8,128)} %get-tuple-element.14) | copy-start | bytes 24580
  158.7 98.9 %copy-start.130 = (f32[16,128]{1,0:T(8,128)S(1)}, f32[16,128]{1,0:T(8,128)}, u32[]{:S(2)}) copy-start(f32[16,128]{1,0:T(8,128)} %get-tuple-element.8) | copy-start | bytes 24580
  158.7 98.9 %copy-start.129 = (f32[16,128]{1,0:T(8,128)S(1)}, f32[16,128]{1,0:T(8,128)}, u32[]{:S(2)}) copy-start(f32[16,128]{1,0:T(8,128)} %get-tuple-element.7) | copy-start | bytes 24580
  158.7 98.9 %copy-start.128 = (f32[16,128]{1,0:T(8,128)S(1)}, f32[16,128]{1,0:T(8,128)}, u32[]{:S(2)}) copy-start(f32[16,128]{1,0:T(8,128)} %get-tuple-element.6) | copy-start | bytes 24580
  241.5 16.1 %collective-permute-start.16 = (f32[21,3,128]{2,0,1:T(8,128)S(1)}, f32[21,3,128]{2,0,1:T(8,128)S(1)}, u32[]{:S(2)}, u32[]{:S(2)}) collective-permute-start(f32[21,3,128]{2,0,1:T(8,128)S(1)} %get-tuple-element.232), channel_id=1, source_target_pairs={{0,16},{16,32},{32,48},{48,64},{64,80},{80,96},{96,112},{112,128},... | collective-permute-start | bytes 96776 | tf_op jit(solution)/shard_map/ppermute | solution.py:22
  243.5 14.2 %collective-permute-start.17 = (f32[21,3,128]{2,0,1:T(8,128)S(1)}, f32[21,3,128]{2,0,1:T(8,128)S(1)}, u32[]{:S(2)}, u32[]{:S(2)}) collective-permute-start(f32[21,3,128]{2,0,1:T(8,128)S(1)} %get-tuple-element.233), channel_id=1, source_target_pairs={{16,0},{32,16},{48,32},{64,48},{80,64},{96,80},{112,96},{128,112},... | collective-permute-start | bytes 96776 | tf_op jit(solution)/shard_map/ppermute | solution.py:25
  257.8 14.9 %collective-permute-start.18 = (f32[21,22,3]{2,0,1:T(8,128)S(1)}, f32[21,22,3]{2,0,1:T(8,128)S(1)}, u32[]{:S(2)}, u32[]{:S(2)}) collective-permute-start(f32[21,22,3]{2,0,1:T(8,128)S(1)} %get-tuple-element.215), channel_id=1, source_target_pairs={{0,1},{1,2},{2,3},{3,4},{4,5},{5,6},{6,7},{7,8},{8,9},{9,10},{10,1... | collective-permute-start | bytes 16640 | tf_op jit(solution)/shard_map/ppermute | solution.py:22
  261.6 14.6 %collective-permute-start.19 = (f32[21,22,3]{2,0,1:T(8,128)S(1)}, f32[21,22,3]{2,0,1:T(8,128)S(1)}, u32[]{:S(2)}, u32[]{:S(2)}) collective-permute-start(f32[21,22,3]{2,0,1:T(8,128)S(1)} %get-tuple-element.216), channel_id=1, source_target_pairs={{1,0},{2,1},{3,2},{4,3},{5,4},{6,5},{7,6},{8,7},{9,8},{10,9},{11,1... | collective-permute-start | bytes 16640 | tf_op jit(solution)/shard_map/ppermute | solution.py:25
  (128 other events, 4384.6 us)
where the time goes:
time: 319 us; the launch traced here: 314 us
  other arithmetic  84.1 us (26%)
  blocking collectives  81.1 us (25%)
  starting transfers between devices  67.7 us (21%)
  waiting for transfers between devices  59.5 us (19%)
  local copies, waits for them, and re-layouts  14.4 us (5%)
  between operations  3.99 us (1%)
  matrix products  3.54 us (1%)
    psum x1, blocking collectives, on_device(): lax.psum(compat_sum, ('rows', 'cols')) / math.sqrt(total_pixels)  81.1 us
    ppermute x10, starting transfers between devices, with_halo(): lax.ppermute(lax.slice_in_dim(block, block.shape[dim] - width, None, axis...  40.5 us
    ppermute x10, waiting for transfers between devices, with_halo(): lax.ppermute(lax.slice_in_dim(block, 0, width, axis=dim), axis, backward)  31.4 us
    ppermute x10, waiting for transfers between devices, with_halo(): lax.ppermute(lax.slice_in_dim(block, block.shape[dim] - width, None, axis...  28.1 us
    ppermute x10, starting transfers between devices, with_halo(): lax.ppermute(lax.slice_in_dim(block, 0, width, axis=dim), axis, backward)  27.2 us
    reduce_sum x16, other arithmetic, pair_terms(): jnp.sum(grad_center * prob_shift + grad_shift * prob_center, axis=0)  16.8 us
    mul x24, other arithmetic, affinity(): spatial_weight(row_step, col_step) * jnp.exp(-distance * factor)  14 us
    sub x1, other arithmetic, softmax_grad(): return prob * (cotangent - jnp.sum(cotangent * prob, axis=0, keepdims=True))  13.9 us
  transfers between devices with their start and end apart: 20, of which 11 were waited for; matrix products, arithmetic and copies ran while one was open for 4% of the time, Pallas kernels for 0%

commit v1 on v0

--- a/solution.py
+++ b/solution.py
@@ -153,7 +153,7 @@
         coefs = coefs + pair_terms(grad_wide, prob_wide)
     unary_grad = unary_sum + softmax_grad(prob_list[0], cotangent)
     feature_grad = feature_term(coefs, kernel_at(), feat_wide)
-    compat_grad = lax.psum(compat_sum, ("rows", "cols")) / math.sqrt(total_pixels)
+    compat_grad = lax.psum(lax.psum(compat_sum, "rows"), "cols") / math.sqrt(total_pixels)
     return (unary_grad, feature_grad, compat_grad)
 
 

time: 319 us -> 368 us (1.15)
  the two profiles are of different devices: /device:TPU:33 before, /device:TPU:129 now
where the time goes in v1:
time: 368 us; the launch traced here: 363 us
  blocking collectives  108 us (29%)
  starting transfers between devices  89.9 us (24%)
  other arithmetic  84.1 us (23%)
  waiting for transfers between devices  59.1 us (16%)
  local copies, waits for them, and re-layouts  14.4 us (4%)
  between operations  4 us (1%)
    psum x1, blocking collectives, on_device(): lax.psum(lax.psum(compat_sum, 'rows'), 'cols') / math.sqrt(total_pixels)  59.3 us
    ppermute x10, starting transfers between devices, with_halo(): lax.ppermute(lax.slice_in_dim(block, block.shape[dim] - width, None, axis...  51.1 us
    psum x1, blocking collectives, on_device(): lax.psum(compat_sum, 'rows')  48.9 us
    ppermute x10, waiting for transfers between devices, with_halo(): lax.ppermute(lax.slice_in_dim(block, 0, width, axis=dim), axis, backward)  40.4 us
    ppermute x10, starting transfers between devices, with_halo(): lax.ppermute(lax.slice_in_dim(block, 0, width, axis=dim), axis, backward)  38.8 us
    ppermute x10, waiting for transfers between devices, with_halo(): lax.ppermute(lax.slice_in_dim(block, block.shape[dim] - width, None, axis...  18.7 us
    reduce_sum x16, other arithmetic, pair_terms(): jnp.sum(grad_center * prob_shift + grad_shift * prob_center, axis=0)  16.8 us
    mul x24, other arithmetic, affinity(): spatial_weight(row_step, col_step) * jnp.exp(-distance * factor)  14 us
  transfers between devices with their start and end apart: 20, of which 11 were waited for; matrix products, arithmetic and copies ran while one was open for 4% of the time, Pallas kernels for 0%

profile of v1, /device:TPU:129, one launch (start us, length us, event | category | flops | bytes accessed | tf_op | source)
XLA Modules:
  0.0 363.2 jit_solution(11681966647966359044)
XLA Ops:
  3.7 3.8 %collective-permute-start.3 = (f32[21,3,128]{2,0,1:T(8,128)S(1)}, f32[21,3,128]{2,0,1:T(8,128)S(1)}, u32[]{:S(2)}, u32[]{:S(2)}) collective-permute-start(f32[21,3,128]{2,0,1:T(8,128)S(1)} %get-tuple-element.238), channel_id=1, source_target_pairs={{0,16},{16,32},{32,48},{48,64},{64,80},{80,96},{96,112},{112,128},... | collective-permute-start | bytes 96776 | tf_op jit(solution)/shard_map/ppermute | solution.py:22
  7.5 1.9 collective-permute-start.4
  9.5 3.6 %collective-permute-start = (bf16[64,3,128]{2,1,0:T(4,128)(2,1)S(1)}, bf16[64,3,128]{2,1,0:T(4,128)(2,1)S(1)}, u32[]{:S(2)}, u32[]{:S(2)}) collective-permute-start(bf16[64,3,128]{2,1,0:T(4,128)(2,1)S(1)} %get-tuple-element.229), channel_id=1, source_target_pairs={{0,16},{16,32},{32,48},{48,64},{64,80},{80,96},{96,112},{112,128},... | collective-permute-start | bytes 147464 | tf_op jit(solution)/shard_map/ppermute | solution.py:22
  13.1 1.9 collective-permute-start.1
  15.2 4.5 %collective-permute-start.5 = (f32[21,22,3]{2,0,1:T(8,128)S(1)}, f32[21,22,3]{2,0,1:T(8,128)S(1)}, u32[]{:S(2)}, u32[]{:S(2)}) collective-permute-start(f32[21,22,3]{2,0,1:T(8,128)S(1)} %get-tuple-element.227), channel_id=1, source_target_pairs={{0,1},{1,2},{2,3},{3,4},{4,5},{5,6},{6,7},{7,8},{8,9},{9,10},{10,1... | collective-permute-start | bytes 16640 | tf_op jit(solution)/shard_map/ppermute | solution.py:22
  19.8 4.4 %collective-permute-start.7 = (f32[21,22,3]{2,0,1:T(8,128)S(1)}, f32[21,22,3]{2,0,1:T(8,128)S(1)}, u32[]{:S(2)}, u32[]{:S(2)}) collective-permute-start(f32[21,22,3]{2,0,1:T(8,128)S(1)} %get-tuple-element.228), channel_id=1, source_target_pairs={{1,0},{2,1},{3,2},{4,3},{5,4},{6,5},{7,6},{8,7},{9,8},{10,9},{11,1... | collective-permute-start | bytes 16640 | tf_op jit(solution)/shard_map/ppermute | solution.py:25
  24.2 7.0 %collective-permute-done.5 = f32[21,22,3]{2,0,1:T(8,128)S(1)} collective-permute-done((f32[21,22,3]{2,0,1:T(8,128)S(1)}, f32[21,22,3]{2,0,1:T(8,128)S(1)}, u32[]{:S(2)}, u32[]{:S(2)}) %collective-permute-start.5) | collective-permute-done | bytes 5576 | tf_op jit(solution)/shard_map/ppermute | solution.py:22
  31.1 3.1 collective-permute-done.7
  34.9 2.5 collective-permute-start.6
  37.4 4.3 %collective-permute-start.2 = (bf16[64,22,3]{2,1,0:T(8,128)(2,1)S(1)}, bf16[64,22,3]{2,1,0:T(8,128)(2,1)S(1)}, u32[]{:S(2)}, u32[]{:S(2)}) collective-permute-start(bf16[64,22,3]{2,1,0:T(8,128)(2,1)S(1)} %get-tuple-element.212), channel_id=1, source_target_pairs={{0,1},{1,2},{2,3},{3,4},{4,5},{5,6},{6,7},{7,8},{8,9},{9,10},{10,1... | collective-permute-start | bytes 25352 | tf_op jit(solution)/shard_map/ppermute | solution.py:22
  41.8 15.3 %collective-permute-done.6 = bf16[64,22,3]{2,1,0:T(8,128)(2,1)S(1)} collective-permute-done((bf16[64,22,3]{2,1,0:T(8,128)(2,1)S(1)}, bf16[64,22,3]{2,1,0:T(8,128)(2,1)S(1)}, u32[]{:S(2)}, u32[]{:S(2)}) %collective-permute-start.6) | collective-permute-done | bytes 8480 | tf_op jit(solution)/shard_map/ppermute | solution.py:25
  58.2 2.4 multiply_reduce_fusion.43
  60.7 2.9 multiply_reduce_fusion.47
  63.6 2.6 multiply_reduce_fusion.46
  80.8 2.7 multiply_add_fusion.4
  84.6 5.8 %collective-permute-start.8 = (f32[21,3,128]{2,0,1:T(8,128)S(1)}, f32[21,3,128]{2,0,1:T(8,128)S(1)}, u32[]{:S(2)}, u32[]{:S(2)}) collective-permute-start(f32[21,3,128]{2,0,1:T(8,128)S(1)} %get-tuple-element.236), channel_id=1, source_target_pairs={{0,16},{16,32},{32,48},{48,64},{64,80},{80,96},{96,112},{112,128},... | collective-permute-start | bytes 96776 | tf_op jit(solution)/shard_map/ppermute | solution.py:22
  90.4 1.9 collective-permute-start.9
  92.3 3.3 collective-permute-done.9
  95.8 3.6 collective-permute-start.10
  99.4 5.5 %collective-permute-start.11 = (f32[21,22,3]{2,0,1:T(8,128)S(1)}, f32[21,22,3]{2,0,1:T(8,128)S(1)}, u32[]{:S(2)}, u32[]{:S(2)}) collective-permute-start(f32[21,22,3]{2,0,1:T(8,128)S(1)} %get-tuple-element.224), channel_id=1, source_target_pairs={{1,0},{2,1},{3,2},{4,3},{5,4},{6,5},{7,6},{8,7},{9,8},{10,9},{11,1... | collective-permute-start | bytes 16640 | tf_op jit(solution)/shard_map/ppermute | solution.py:25
  104.9 4.9 %collective-permute-done.10 = f32[21,22,3]{2,0,1:T(8,128)S(1)} collective-permute-done((f32[21,22,3]{2,0,1:T(8,128)S(1)}, f32[21,22,3]{2,0,1:T(8,128)S(1)}, u32[]{:S(2)}, u32[]{:S(2)}) %collective-permute-start.10) | collective-permute-done | bytes 5576 | tf_op jit(solution)/shard_map/ppermute | solution.py:22
  109.8 4.0 %collective-permute-done.11 = f32[21,22,3]{2,0,1:T(8,128)S(1)} collective-permute-done((f32[21,22,3]{2,0,1:T(8,128)S(1)}, f32[21,22,3]{2,0,1:T(8,128)S(1)}, u32[]{:S(2)}, u32[]{:S(2)}) %collective-permute-start.11) | collective-permute-done | bytes 5576 | tf_op jit(solution)/shard_map/ppermute | solution.py:25
  114.0 2.8 multiply_add_fusion.3
  120.9 4.6 %collective-permute-start.12 = (f32[21,3,128]{2,0,1:T(8,128)S(1)}, f32[21,3,128]{2,0,1:T(8,128)S(1)}, u32[]{:S(2)}, u32[]{:S(2)}) collective-permute-start(f32[21,3,128]{2,0,1:T(8,128)S(1)} %get-tuple-element.234), channel_id=1, source_target_pairs={{0,16},{16,32},{32,48},{48,64},{64,80},{80,96},{96,112},{112,128},... | collective-permute-start | bytes 96776 | tf_op jit(solution)/shard_map/ppermute | solution.py:22
  125.5 1.9 collective-permute-start.13
  127.4 3.3 collective-permute-done.13
  130.9 1.9 collective-permute-start.14
  132.8 7.0 %collective-permute-start.15 = (f32[21,22,3]{2,0,1:T(8,128)S(1)}, f32[21,22,3]{2,0,1:T(8,128)S(1)}, u32[]{:S(2)}, u32[]{:S(2)}) collective-permute-start(f32[21,22,3]{2,0,1:T(8,128)S(1)} %get-tuple-element.220), channel_id=1, source_target_pairs={{1,0},{2,1},{3,2},{4,3},{5,4},{6,5},{7,6},{8,7},{9,8},{10,9},{11,1... | collective-permute-start | bytes 16640 | tf_op jit(solution)/shard_map/ppermute | solution.py:25
  140.5 2.5 collective-permute-done.14
  143.1 5.8 %collective-permute-done.15 = f32[21,22,3]{2,0,1:T(8,128)S(1)} collective-permute-done((f32[21,22,3]{2,0,1:T(8,128)S(1)}, f32[21,22,3]{2,0,1:T(8,128)S(1)}, u32[]{:S(2)}, u32[]{:S(2)}) %collective-permute-start.15) | collective-permute-done | bytes 5576 | tf_op jit(solution)/shard_map/ppermute | solution.py:25
  150.3 1.5 add_reduce_fusion.64
  155.7 4.4 %add_reduce_fusion.48 = (f32[16,128]{1,0:T(8,128)}, f32[16,128]{1,0:T(8,128)}, f32[16,128]{1,0:T(8,128)}, f32[16,128]{1,0:T(8,128)}, f32[16,128]{1,0:T(8,128)}, ...) fusion(f32[21,16,128]{2,0,1:T(8,128)S(1)} %fusion.11, ...), kind=kLoop, calls=%fused_computation.349 | loop fusion | flops 5830656 | bytes 9657344 | tf_op jit(solution)/shard_map/reduce_sum | solution.py:77
  163.4 48.9 %psum.14 = f32[21,21]{1,0:T(8,128)S(1)} all-reduce(f32[21,21]{1,0:T(8,128)S(1)} %fusion.15), channel_id=1, replica_groups=mesh['rows'=16,'cols'=16] {'rows'}, use_global_device_ids=true, to_apply=%region_153.0 | all-reduce | flops 441 | bytes 3528 | tf_op jit(solution)/shard_map/psum | solution.py:156
  212.3 59.3 %psum.15 = f32[21,21]{1,0:T(8,128)S(1)} all-reduce(f32[21,21]{1,0:T(8,128)S(1)} %psum.14), channel_id=1, replica_groups=mesh['rows'=16,'cols'=16] {'cols'}, use_global_device_ids=true, to_apply=%region_154.0 | all-reduce | flops 441 | bytes 3528 | tf_op jit(solution)/shard_map/psum | solution.py:156
  272.2 17.1 %collective-permute-start.16 = (f32[21,3,128]{2,0,1:T(8,128)S(1)}, f32[21,3,128]{2,0,1:T(8,128)S(1)}, u32[]{:S(2)}, u32[]{:S(2)}) collective-permute-start(f32[21,3,128]{2,0,1:T(8,128)S(1)} %get-tuple-element.232), channel_id=1, source_target_pairs={{0,16},{16,32},{32,48},{48,64},{64,80},{80,96},{96,112},{112,128},... | collective-permute-start | bytes 96776 | tf_op jit(solution)/shard_map/ppermute | solution.py:22
  289.3 4.6 %collective-permute-start.17 = (f32[21,3,128]{2,0,1:T(8,128)S(1)}, f32[21,3,128]{2,0,1:T(8,128)S(1)}, u32[]{:S(2)}, u32[]{:S(2)}) collective-permute-start(f32[21,3,128]{2,0,1:T(8,128)S(1)} %get-tuple-element.233), channel_id=1, source_target_pairs={{16,0},{32,16},{48,32},{64,48},{80,64},{96,80},{112,96},{128,112},... | collective-permute-start | bytes 96776 | tf_op jit(solution)/shard_map/ppermute | solution.py:25
  305.9 1.9 collective-permute-start.18
  307.8 7.2 %collective-permute-start.19 = (f32[21,22,3]{2,0,1:T(8,128)S(1)}, f32[21,22,3]{2,0,1:T(8,128)S(1)}, u32[]{:S(2)}, u32[]{:S(2)}) collective-permute-start(f32[21,22,3]{2,0,1:T(8,128)S(1)} %get-tuple-element.216), channel_id=1, source_target_pairs={{1,0},{2,1},{3,2},{4,3},{5,4},{6,5},{7,6},{8,7},{9,8},{10,9},{11,1... | collective-permute-start | bytes 16640 | tf_op jit(solution)/shard_map/ppermute | solution.py:25
  315.3 4.3 %collective-permute-done.18 = f32[21,22,3]{2,0,1:T(8,128)S(1)} collective-permute-done((f32[21,22,3]{2,0,1:T(8,128)S(1)}, f32[21,22,3]{2,0,1:T(8,128)S(1)}, u32[]{:S(2)}, u32[]{:S(2)}) %collective-permute-start.18) | collective-permute-done | bytes 5576 | tf_op jit(solution)/shard_map/ppermute | solution.py:22
  319.6 5.6 %collective-permute-done.19 = f32[21,22,3]{2,0,1:T(8,128)S(1)} collective-permute-done((f32[21,22,3]{2,0,1:T(8,128)S(1)}, f32[21,22,3]{2,0,1:T(8,128)S(1)}, u32[]{:S(2)}, u32[]{:S(2)}) %collective-permute-start.19) | collective-permute-done | bytes 5576 | tf_op jit(solution)/shard_map/ppermute | solution.py:25
  330.8 1.4 fusion.129
  332.2 1.4 fusion.131
  333.7 1.4 fusion.133
  335.2 1.4 fusion.135
  336.6 1.4 fusion.137
  338.1 1.5 fusion.139
  339.9 13.9 %fusion.7 = f32[21,16,128]{2,0,1:T(8,128)S(1)} fusion(f32[21,16,128]{2,0,1:T(8,128)S(1)} %copy-done.10, f32[16,128]{1,0:T(8,128)} %fusion.19, f32[21,16,128]{2,1,0:T(8,128)} %param.7, f32[21,16,128]{2,0,1:T(8,128)} %copy-done.11, f32[16,128]{1,0:T(8,128)} %get-tuple-element.242, f32[16,128]{1,0:T(8,128)S(1)} %copy-done.13, f32[16,128]{1,0:T(8,128)S(1)} %reduce_max.27, ...), kind=kOutput, calls=%fused_computation.55 | output fusion | flops 9205780 | bytes 18972672 | tf_op jit(solution)/shard_map/sub | solution.py:109
  354.9 8.3 %multiply_add_fusion = f32[64,16,128]{2,1,0:T(8,128)} fusion(bf16[64,16,128]{2,1,0:T(8,128)(2,1)S(1)} %copy-done.6, bf16[64,3,128]{2,1,0:T(4,128)(2,1)S(1)} %collective-permute-done, f32[16,128]{1,0:T(8,128)} %get-tuple-element.162, f32[16,128]{1,0:T(8,128)} %get-tuple-element.163, f32[16,128]{1,0:T(8,128)} %get-tuple-element.164, ...), kind=kLoop, calls=%fused_computation.80 | loop fusion | flops 26345472 | bytes 13025280 | tf_op jit(solution)/shard_map/add | solution.py:92
  (493 shorter events, 51.8 us)
Async XLA Ops:
  3.7 11.4 %collective-permute-start.3 = (f32[21,3,128]{2,0,1:T(8,128)S(1)}, f32[21,3,128]{2,0,1:T(8,128)S(1)}, u32[]{:S(2)}, u32[]{:S(2)}) collective-permute-start(f32[21,3,128]{2,0,1:T(8,128)S(1)} %get-tuple-element.238), channel_id=1, source_target_pairs={{0,16},{16,32},{32,48},{48,64},{64,80},{80,96},{96,112},{112,128},... | collective-permute-start | bytes 96776 | tf_op jit(solution)/shard_map/ppermute | solution.py:22
  7.5 7.6 %collective-permute-start.4 = (f32[21,3,128]{2,0,1:T(8,128)S(1)}, f32[21,3,128]{2,0,1:T(8,128)S(1)}, u32[]{:S(2)}, u32[]{:S(2)}) collective-permute-start(f32[21,3,128]{2,0,1:T(8,128)S(1)} %get-tuple-element.239), channel_id=1, source_target_pairs={{16,0},{32,16},{48,32},{64,48},{80,64},{96,80},{112,96},{128,112},... | collective-permute-start | bytes 96776 | tf_op jit(solution)/shard_map/ppermute | solution.py:25
  9.5 25.0 %collective-permute-start = (bf16[64,3,128]{2,1,0:T(4,128)(2,1)S(1)}, bf16[64,3,128]{2,1,0:T(4,128)(2,1)S(1)}, u32[]{:S(2)}, u32[]{:S(2)}) collective-permute-start(bf16[64,3,128]{2,1,0:T(4,128)(2,1)S(1)} %get-tuple-element.229), channel_id=1, source_target_pairs={{0,16},{16,32},{32,48},{48,64},{64,80},{80,96},{96,112},{112,128},... | collective-permute-start | bytes 147464 | tf_op jit(solution)/shard_map/ppermute | solution.py:22
  13.1 21.4 %collective-permute-start.1 = (bf16[64,3,128]{2,1,0:T(4,128)(2,1)S(1)}, bf16[64,3,128]{2,1,0:T(4,128)(2,1)S(1)}, u32[]{:S(2)}, u32[]{:S(2)}) collective-permute-start(bf16[64,3,128]{2,1,0:T(4,128)(2,1)S(1)} %get-tuple-element.230), channel_id=1, source_target_pairs={{16,0},{32,16},{48,32},{64,48},{80,64},{96,80},{112,96},{128,112},... | collective-permute-start | bytes 147464 | tf_op jit(solution)/shard_map/ppermute | solution.py:25
  15.2 15.9 %collective-permute-start.5 = (f32[21,22,3]{2,0,1:T(8,128)S(1)}, f32[21,22,3]{2,0,1:T(8,128)S(1)}, u32[]{:S(2)}, u32[]{:S(2)}) collective-permute-start(f32[21,22,3]{2,0,1:T(8,128)S(1)} %get-tuple-element.227), channel_id=1, source_target_pairs={{0,1},{1,2},{2,3},{3,4},{4,5},{5,6},{6,7},{7,8},{8,9},{9,10},{10,1... | collective-permute-start | bytes 16640 | tf_op jit(solution)/shard_map/ppermute | solution.py:22
  19.8 14.5 %collective-permute-start.7 = (f32[21,22,3]{2,0,1:T(8,128)S(1)}, f32[21,22,3]{2,0,1:T(8,128)S(1)}, u32[]{:S(2)}, u32[]{:S(2)}) collective-permute-start(f32[21,22,3]{2,0,1:T(8,128)S(1)} %get-tuple-element.228), channel_id=1, source_target_pairs={{1,0},{2,1},{3,2},{4,3},{5,4},{6,5},{7,6},{8,7},{9,8},{10,9},{11,1... | collective-permute-start | bytes 16640 | tf_op jit(solution)/shard_map/ppermute | solution.py:25
  34.9 22.1 %collective-permute-start.6 = (bf16[64,22,3]{2,1,0:T(8,128)(2,1)S(1)}, bf16[64,22,3]{2,1,0:T(8,128)(2,1)S(1)}, u32[]{:S(2)}, u32[]{:S(2)}) collective-permute-start(bf16[64,22,3]{2,1,0:T(8,128)(2,1)S(1)} %get-tuple-element.211), channel_id=1, source_target_pairs={{1,0},{2,1},{3,2},{4,3},{5,4},{6,5},{7,6},{8,7},{9,8},{10,9},{11,1... | collective-permute-start | bytes 25352 | tf_op jit(solution)/shard_map/ppermute | solution.py:25
  37.4 19.6 %collective-permute-start.2 = (bf16[64,22,3]{2,1,0:T(8,128)(2,1)S(1)}, bf16[64,22,3]{2,1,0:T(8,128)(2,1)S(1)}, u32[]{:S(2)}, u32[]{:S(2)}) collective-permute-start(bf16[64,22,3]{2,1,0:T(8,128)(2,1)S(1)} %get-tuple-element.212), channel_id=1, source_target_pairs={{0,1},{1,2},{2,3},{3,4},{4,5},{5,6},{6,7},{7,8},{8,9},{9,10},{10,1... | collective-permute-start | bytes 25352 | tf_op jit(solution)/shard_map/ppermute | solution.py:22
  84.6 7.7 %collective-permute-start.8 = (f32[21,3,128]{2,0,1:T(8,128)S(1)}, f32[21,3,128]{2,0,1:T(8,128)S(1)}, u32[]{:S(2)}, u32[]{:S(2)}) collective-permute-start(f32[21,3,128]{2,0,1:T(8,128)S(1)} %get-tuple-element.236), channel_id=1, source_target_pairs={{0,16},{16,32},{32,48},{48,64},{64,80},{80,96},{96,112},{112,128},... | collective-permute-start | bytes 96776 | tf_op jit(solution)/shard_map/ppermute | solution.py:22
  90.4 5.3 %collective-permute-start.9 = (f32[21,3,128]{2,0,1:T(8,128)S(1)}, f32[21,3,128]{2,0,1:T(8,128)S(1)}, u32[]{:S(2)}, u32[]{:S(2)}) collective-permute-start(f32[21,3,128]{2,0,1:T(8,128)S(1)} %get-tuple-element.237), channel_id=1, source_target_pairs={{16,0},{32,16},{48,32},{64,48},{80,64},{96,80},{112,96},{128,112},... | collective-permute-start | bytes 96776 | tf_op jit(solution)/shard_map/ppermute | solution.py:25
  95.8 14.0 %collective-permute-start.10 = (f32[21,22,3]{2,0,1:T(8,128)S(1)}, f32[21,22,3]{2,0,1:T(8,128)S(1)}, u32[]{:S(2)}, u32[]{:S(2)}) collective-permute-start(f32[21,22,3]{2,0,1:T(8,128)S(1)} %get-tuple-element.223), channel_id=1, source_target_pairs={{0,1},{1,2},{2,3},{3,4},{4,5},{5,6},{6,7},{7,8},{8,9},{9,10},{10,1... | collective-permute-start | bytes 16640 | tf_op jit(solution)/shard_map/ppermute | solution.py:22
  99.4 14.4 %collective-permute-start.11 = (f32[21,22,3]{2,0,1:T(8,128)S(1)}, f32[21,22,3]{2,0,1:T(8,128)S(1)}, u32[]{:S(2)}, u32[]{:S(2)}) collective-permute-start(f32[21,22,3]{2,0,1:T(8,128)S(1)} %get-tuple-element.224), channel_id=1, source_target_pairs={{1,0},{2,1},{3,2},{4,3},{5,4},{6,5},{7,6},{8,7},{9,8},{10,9},{11,1... | collective-permute-start | bytes 16640 | tf_op jit(solution)/shard_map/ppermute | solution.py:25
  120.9 6.5 %collective-permute-start.12 = (f32[21,3,128]{2,0,1:T(8,128)S(1)}, f32[21,3,128]{2,0,1:T(8,128)S(1)}, u32[]{:S(2)}, u32[]{:S(2)}) collective-permute-start(f32[21,3,128]{2,0,1:T(8,128)S(1)} %get-tuple-element.234), channel_id=1, source_target_pairs={{0,16},{16,32},{32,48},{48,64},{64,80},{80,96},{96,112},{112,128},... | collective-permute-start | bytes 96776 | tf_op jit(solution)/shard_map/ppermute | solution.py:22
  125.5 5.3 %collective-permute-start.13 = (f32[21,3,128]{2,0,1:T(8,128)S(1)}, f32[21,3,128]{2,0,1:T(8,128)S(1)}, u32[]{:S(2)}, u32[]{:S(2)}) collective-permute-start(f32[21,3,128]{2,0,1:T(8,128)S(1)} %get-tuple-element.235), channel_id=1, source_target_pairs={{16,0},{32,16},{48,32},{64,48},{80,64},{96,80},{112,96},{128,112},... | collective-permute-start | bytes 96776 | tf_op jit(solution)/shard_map/ppermute | solution.py:25
  130.9 12.2 %collective-permute-start.14 = (f32[21,22,3]{2,0,1:T(8,128)S(1)}, f32[21,22,3]{2,0,1:T(8,128)S(1)}, u32[]{:S(2)}, u32[]{:S(2)}) collective-permute-start(f32[21,22,3]{2,0,1:T(8,128)S(1)} %get-tuple-element.219), channel_id=1, source_target_pairs={{0,1},{1,2},{2,3},{3,4},{4,5},{5,6},{6,7},{7,8},{8,9},{9,10},{10,1... | collective-permute-start | bytes 16640 | tf_op jit(solution)/shard_map/ppermute | solution.py:22
  132.8 16.0 %collective-permute-start.15 = (f32[21,22,3]{2,0,1:T(8,128)S(1)}, f32[21,22,3]{2,0,1:T(8,128)S(1)}, u32[]{:S(2)}, u32[]{:S(2)}) collective-permute-start(f32[21,22,3]{2,0,1:T(8,128)S(1)} %get-tuple-element.220), channel_id=1, source_target_pairs={{1,0},{2,1},{3,2},{4,3},{5,4},{6,5},{7,6},{8,7},{9,8},{10,9},{11,1... | collective-permute-start | bytes 16640 | tf_op jit(solution)/shard_map/ppermute | solution.py:25
  162.0 141.7 %copy-start.138 = (f32[16,128]{1,0:T(8,128)S(1)}, f32[16,128]{1,0:T(8,128)}, u32[]{:S(2)}) copy-start(f32[16,128]{1,0:T(8,128)} %get-tuple-element.144) | copy-start | bytes 24580
  162.0 141.7 %copy-start.149 = (f32[16,128]{1,0:T(8,128)S(1)}, f32[16,128]{1,0:T(8,128)}, u32[]{:S(2)}) copy-start(f32[16,128]{1,0:T(8,128)} %get-tuple-element.28) | copy-start | bytes 24580
  162.0 141.7 %copy-start.148 = (f32[16,128]{1,0:T(8,128)S(1)}, f32[16,128]{1,0:T(8,128)}, u32[]{:S(2)}) copy-start(f32[16,128]{1,0:T(8,128)} %get-tuple-element.27) | copy-start | bytes 24580
  162.0 141.7 %copy-start.147 = (f32[16,128]{1,0:T(8,128)S(1)}, f32[16,128]{1,0:T(8,128)}, u32[]{:S(2)}) copy-start(f32[16,128]{1,0:T(8,128)} %get-tuple-element.26) | copy-start | bytes 24580
  162.0 143.1 %copy-start.154 = (f32[16,128]{1,0:T(8,128)S(1)}, f32[16,128]{1,0:T(8,128)}, u32[]{:S(2)}) copy-start(f32[16,128]{1,0:T(8,128)} %get-tuple-element.31) | copy-start | bytes 24580
  162.1 143.1 %copy-start.143 = (f32[16,128]{1,0:T(8,128)S(1)}, f32[16,128]{1,0:T(8,128)}, u32[]{:S(2)}) copy-start(f32[16,128]{1,0:T(8,128)} %get-tuple-element.25) | copy-start | bytes 24580
  162.1 143.1 %copy-start.141 = (f32[16,128]{1,0:T(8,128)S(1)}, f32[16,128]{1,0:T(8,128)}, u32[]{:S(2)}) copy-start(f32[16,128]{1,0:T(8,128)} %get-tuple-element.24) | copy-start | bytes 24580
  162.1 143.1 %copy-start.139 = (f32[16,128]{1,0:T(8,128)S(1)}, f32[16,128]{1,0:T(8,128)}, u32[]{:S(2)}) copy-start(f32[16,128]{1,0:T(8,128)} %get-tuple-element.23) | copy-start | bytes 24580
  162.1 143.2 %copy-start.151 = (f32[16,128]{1,0:T(8,128)S(1)}, f32[16,128]{1,0:T(8,128)}, u32[]{:S(2)}) copy-start(f32[16,128]{1,0:T(8,128)} %get-tuple-element.30) | copy-start | bytes 24580
  162.1 143.2 %copy-start.142 = (f32[16,128]{1,0:T(8,128)S(1)}, f32[16,128]{1,0:T(8,128)}, u32[]{:S(2)}) copy-start(f32[16,128]{1,0:T(8,128)} %get-tuple-element.21) | copy-start | bytes 24580
  162.1 143.2 %copy-start.140 = (f32[16,128]{1,0:T(8,128)S(1)}, f32[16,128]{1,0:T(8,128)}, u32[]{:S(2)}) copy-start(f32[16,128]{1,0:T(8,128)} %get-tuple-element.20) | copy-start | bytes 24580
  162.1 143.2 %copy-start.152 = (f32[16,128]{1,0:T(8,128)S(1)}, f32[16,128]{1,0:T(8,128)}, u32[]{:S(2)}) copy-start(f32[16,128]{1,0:T(8,128)} %get-tuple-element.143) | copy-start | bytes 24580
  162.1 143.2 %copy-start.133 = (f32[16,128]{1,0:T(8,128)S(1)}, f32[16,128]{1,0:T(8,128)}, u32[]{:S(2)}) copy-start(f32[16,128]{1,0:T(8,128)} %get-tuple-element.22) | copy-start | bytes 24580
  162.1 143.2 %copy-start.145 = (f32[16,128]{1,0:T(8,128)S(1)}, f32[16,128]{1,0:T(8,128)}, u32[]{:S(2)}) copy-start(f32[16,128]{1,0:T(8,128)} %get-tuple-element.13) | copy-start | bytes 24580
  162.1 143.2 %copy-start.144 = (f32[16,128]{1,0:T(8,128)S(1)}, f32[16,128]{1,0:T(8,128)}, u32[]{:S(2)}) copy-start(f32[16,128]{1,0:T(8,128)} %get-tuple-element.12) | copy-start | bytes 24580
  162.2 143.2 %copy-start.134 = (f32[16,128]{1,0:T(8,128)S(1)}, f32[16,128]{1,0:T(8,128)}, u32[]{:S(2)}) copy-start(f32[16,128]{1,0:T(8,128)} %get-tuple-element.19) | copy-start | bytes 24580
  162.2 143.2 %copy-start.132 = (f32[16,128]{1,0:T(8,128)S(1)}, f32[16,128]{1,0:T(8,128)}, u32[]{:S(2)}) copy-start(f32[16,128]{1,0:T(8,128)} %get-tuple-element.18) | copy-start | bytes 24580
  162.2 143.3 %copy-start.131 = (f32[16,128]{1,0:T(8,128)S(1)}, f32[16,128]{1,0:T(8,128)}, u32[]{:S(2)}) copy-start(f32[16,128]{1,0:T(8,128)} %get-tuple-element.17) | copy-start | bytes 24580
  162.2 143.3 %copy-start.146 = (f32[16,128]{1,0:T(8,128)S(1)}, f32[16,128]{1,0:T(8,128)}, u32[]{:S(2)}) copy-start(f32[16,128]{1,0:T(8,128)} %get-tuple-element.142) | copy-start | bytes 24580
  162.2 143.3 %copy-start.137 = (f32[16,128]{1,0:T(8,128)S(1)}, f32[16,128]{1,0:T(8,128)}, u32[]{:S(2)}) copy-start(f32[16,128]{1,0:T(8,128)} %get-tuple-element.11) | copy-start | bytes 24580
  162.2 143.3 %copy-start.136 = (f32[16,128]{1,0:T(8,128)S(1)}, f32[16,128]{1,0:T(8,128)}, u32[]{:S(2)}) copy-start(f32[16,128]{1,0:T(8,128)} %get-tuple-element.10) | copy-start | bytes 24580
  162.2 143.3 %copy-start.135 = (f32[16,128]{1,0:T(8,128)S(1)}, f32[16,128]{1,0:T(8,128)}, u32[]{:S(2)}) copy-start(f32[16,128]{1,0:T(8,128)} %get-tuple-element.9) | copy-start | bytes 24580
  162.2 143.3 %copy-start.127 = (f32[16,128]{1,0:T(8,128)S(1)}, f32[16,128]{1,0:T(8,128)}, u32[]{:S(2)}) copy-start(f32[16,128]{1,0:T(8,128)} %get-tuple-element.16) | copy-start | bytes 24580
  162.2 143.3 %copy-start.126 = (f32[16,128]{1,0:T(8,128)S(1)}, f32[16,128]{1,0:T(8,128)}, u32[]{:S(2)}) copy-start(f32[16,128]{1,0:T(8,128)} %get-tuple-element.15) | copy-start | bytes 24580
  162.2 143.3 %copy-start.125 = (f32[16,128]{1,0:T(8,128)S(1)}, f32[16,128]{1,0:T(8,128)}, u32[]{:S(2)}) copy-start(f32[16,128]{1,0:T(8,128)} %get-tuple-element.14) | copy-start | bytes 24580
  162.3 143.4 %copy-start.130 = (f32[16,128]{1,0:T(8,128)S(1)}, f32[16,128]{1,0:T(8,128)}, u32[]{:S(2)}) copy-start(f32[16,128]{1,0:T(8,128)} %get-tuple-element.8) | copy-start | bytes 24580
  162.3 143.4 %copy-start.129 = (f32[16,128]{1,0:T(8,128)S(1)}, f32[16,128]{1,0:T(8,128)}, u32[]{:S(2)}) copy-start(f32[16,128]{1,0:T(8,128)} %get-tuple-element.7) | copy-start | bytes 24580
  162.3 143.4 %copy-start.128 = (f32[16,128]{1,0:T(8,128)S(1)}, f32[16,128]{1,0:T(8,128)}, u32[]{:S(2)}) copy-start(f32[16,128]{1,0:T(8,128)} %get-tuple-element.6) | copy-start | bytes 24580
  272.2 33.5 %collective-permute-start.16 = (f32[21,3,128]{2,0,1:T(8,128)S(1)}, f32[21,3,128]{2,0,1:T(8,128)S(1)}, u32[]{:S(2)}, u32[]{:S(2)}) collective-permute-start(f32[21,3,128]{2,0,1:T(8,128)S(1)} %get-tuple-element.232), channel_id=1, source_target_pairs={{0,16},{16,32},{32,48},{48,64},{64,80},{80,96},{96,112},{112,128},... | collective-permute-start | bytes 96776 | tf_op jit(solution)/shard_map/ppermute | solution.py:22
  289.3 16.4 %collective-permute-start.17 = (f32[21,3,128]{2,0,1:T(8,128)S(1)}, f32[21,3,128]{2,0,1:T(8,128)S(1)}, u32[]{:S(2)}, u32[]{:S(2)}) collective-permute-start(f32[21,3,128]{2,0,1:T(8,128)S(1)} %get-tuple-element.233), channel_id=1, source_target_pairs={{16,0},{32,16},{48,32},{64,48},{80,64},{96,80},{112,96},{128,112},... | collective-permute-start | bytes 96776 | tf_op jit(solution)/shard_map/ppermute | solution.py:25
  305.9 13.7 %collective-permute-start.18 = (f32[21,22,3]{2,0,1:T(8,128)S(1)}, f32[21,22,3]{2,0,1:T(8,128)S(1)}, u32[]{:S(2)}, u32[]{:S(2)}) collective-permute-start(f32[21,22,3]{2,0,1:T(8,128)S(1)} %get-tuple-element.215), channel_id=1, source_target_pairs={{0,1},{1,2},{2,3},{3,4},{4,5},{5,6},{6,7},{7,8},{8,9},{9,10},{10,1... | collective-permute-start | bytes 16640 | tf_op jit(solution)/shard_map/ppermute | solution.py:22
  307.8 17.4 %collective-permute-start.19 = (f32[21,22,3]{2,0,1:T(8,128)S(1)}, f32[21,22,3]{2,0,1:T(8,128)S(1)}, u32[]{:S(2)}, u32[]{:S(2)}) collective-permute-start(f32[21,22,3]{2,0,1:T(8,128)S(1)} %get-tuple-element.216), channel_id=1, source_target_pairs={{1,0},{2,1},{3,2},{4,3},{5,4},{6,5},{7,6},{8,7},{9,8},{10,9},{11,1... | collective-permute-start | bytes 16640 | tf_op jit(solution)/shard_map/ppermute | solution.py:25
  (128 other events, 4612.0 us)
